TPU v7x, 32 devices: a whole 2x2x4 slice. The times are simulated.
32 devices in a mesh: batch: 8 (over y, x, core), mp: 4 (over z).
Axes of the slice: x: 2, y: 2, z: 4, core: 2. Of those that a mesh axis runs over, the one named last changes fastest.
Arguments:
- token_ids: int32 [8, 1536], P('batch'), may hold values from 0 to 30527
- segment_ids: int32 [8, 1536], P('batch'), may hold values from 0 to 8, never falling along the last dimension, each value on 1 to 1024 neighbouring positions
- row_of: int32 [30528], replicated, may hold values from 0 to 30527, each once
- query_count: int32 [1], replicated, may hold values from 16 to 32
- table: float32 [30528, 768], P('batch'), may hold values from -8 to 8
- qkv_weight: float32 [768, 3, 768], P('batch', None, 'mp'), may hold values from -0.21875 to 0.21875
- out_weight: float32 [768, 768], P('mp', 'batch'), may hold values from -0.875 to 0.875
- gate_up_weight: float32 [768, 2, 3072], P('batch', None, 'mp'), may hold values from -0.21875 to 0.21875
- down_weight: float32 [3072, 768], P('mp', 'batch'), may hold values from -0.109375 to 0.109375
- gains: float32 [2, 768], P(None, 'batch'), may hold values from 0.3 to 2.5
- table_m: float32 [30528, 768], P('batch'), may hold values from -0.0009765625 to 0.0009765625
- qkv_m: float32 [768, 3, 768], P('batch', None, 'mp'), may hold values from -0.0009765625 to 0.0009765625
- out_m: float32 [768, 768], P('mp', 'batch'), may hold values from -0.0009765625 to 0.0009765625
- gate_up_m: float32 [768, 2, 3072], P('batch', None, 'mp'), may hold values from -0.0009765625 to 0.0009765625
- down_m: float32 [3072, 768], P('mp', 'batch'), may hold values from -0.0009765625 to 0.0009765625
- gains_m: float32 [2, 768], P(None, 'batch'), may hold values from -0.0009765625 to 0.0009765625
- table_v: float32 [30528, 768], P('batch'), may hold values from 3.040972e-08 to 1.2163888e-07
- qkv_v: float32 [768, 3, 768], P('batch', None, 'mp'), may hold values from 3.040972e-08 to 1.2163888e-07
- out_v: float32 [768, 768], P('mp', 'batch'), may hold values from 3.040972e-08 to 1.2163888e-07
- gate_up_v: float32 [768, 2, 3072], P('batch', None, 'mp'), may hold values from 3.040972e-08 to 1.2163888e-07
- down_v: float32 [3072, 768], P('mp', 'batch'), may hold values from 3.040972e-08 to 1.2163888e-07
- gains_v: float32 [2, 768], P(None, 'batch'), may hold values from 3.040972e-08 to 1.2163888e-07
Outputs:
- loss: float32 [1], replicated
- grad_norm: float32 [1], replicated
- new_table: float32 [30528, 768], P('batch')
- new_qkv_weight: float32 [768, 3, 768], P('batch', None, 'mp')
- new_out_weight: float32 [768, 768], P('mp', 'batch')
- new_gate_up_weight: float32 [768, 2, 3072], P('batch', None, 'mp')
- new_down_weight: float32 [3072, 768], P('mp', 'batch')
- new_gains: float32 [2, 768], P(None, 'batch')
- clipped_table_grad: float32 [30528, 768], P('batch')
- new_qkv_m: float32 [768, 3, 768], P('batch', None, 'mp')
- new_out_m: float32 [768, 768], P('mp', 'batch')
- new_gate_up_m: float32 [768, 2, 3072], P('batch', None, 'mp')
- new_down_m: float32 [3072, 768], P('mp', 'batch')
- new_gains_m: float32 [2, 768], P(None, 'batch')
- new_table_v: float32 [30528, 768], P('batch')
- new_qkv_v: float32 [768, 3, 768], P('batch', None, 'mp')
- new_out_v: float32 [768, 768], P('mp', 'batch')
- new_gate_up_v: float32 [768, 2, 3072], P('batch', None, 'mp')
- new_down_v: float32 [3072, 768], P('mp', 'batch')
- new_gains_v: float32 [2, 768], P(None, 'batch')
Inputs may be any that keep to these rules, and one draw needn't show every extreme that they name: `segment_ids`: in each row the ids never fall, every id 0 to 8 appears, id 8 marks padding, each segment has 1 to 1024 tokens and one has exactly 1024. A permutation: token t's embedding is table row row_of[t]. The first query_count queries count.
All inputs are finite; a program needn't handle non-finite values.
Results may differ from a plain program's by a relative error of at most 0.0075.
The roundings to bfloat16 on the way count: a program that leaves them out, or rounds other values in their place, can miss the bound.
Values may be sent and summed in bfloat16 or wider, within the bound.
A program may use at most 320 MiB of HBM per device.

v0:
```python
from functools import partial
import jax
import jax.numpy as jnp
from jax import lax
from jax.sharding import PartitionSpec as P

D = 768
HEAD_DIM = 64
SEGS = 8
peak_affinity = lax.Precision.HIGHEST
sharpness_divisor = 0.05
clip_limit = 1.0
step_number = 3.0
rates = (0.3, 0.02, 0.02, 0.02, 0.02, 0.3)
negative = -1e30


def positions(segment_row, segment_count):
    labels = jnp.arange(segment_count + 1, dtype=jnp.int32)
    member = (segment_row[:, None] == labels[None, :]).astype(jnp.int32)
    counts = jnp.sum(member, 0)
    starts = jnp.cumsum(counts) - counts
    first_index = jnp.sum(member * starts[None, :], 1)
    return (jnp.arange(segment_row.shape[0], dtype=jnp.int32) - first_index).astype(jnp.float32)


def rotate(values, places):
    half_dim = values.shape[-1] // 2
    freqs = jnp.power(1000.0, -2.0 * jnp.arange(half_dim, dtype=jnp.float32) / values.shape[-1])
    angles = places[:, None] * freqs[None, :]
    cosine = jnp.cos(angles)[:, None, :]
    sine = jnp.sin(angles)[:, None, :]
    former = values[..., :half_dim]
    latter = values[..., half_dim:]
    return jnp.concatenate([former * cosine - latter * sine, latter * cosine + former * sine], -1)


def layer_norm(values, gain):
    centred = values - jnp.mean(values, -1, keepdims=True)
    spread = jnp.mean(centred * centred, -1, keepdims=True)
    return centred * lax.rsqrt(spread + 1e-05) * gain


def swiglu(gate_up):
    return jax.nn.silu(gate_up[:, 0]) * gate_up[:, 1]


def contract(left, right, left_dim, right_dim):
    return lax.dot_general(
        left, right, (((left_dim,), (right_dim,)), ((), ())), preferred_element_type=jnp.float32
    )


def pool_rows(hidden, segment_ids):
    rows_dev, length = segment_ids.shape
    labels = jnp.arange(SEGS, dtype=jnp.int32)
    member = (segment_ids[:, None, :] == labels[None, :, None]).astype(jnp.float32)
    sums = jnp.einsum(
        "rsl,rld->rsd", member, hidden.reshape(rows_dev, length, -1), precision=peak_affinity
    )
    pooled = (sums / jnp.sum(member, -1, keepdims=True)).reshape(rows_dev * SEGS, -1)
    return pooled * lax.rsqrt(jnp.sum(pooled * pooled, -1, keepdims=True) + 1e-06)


def block_scores(query_block, key_row, segment_block, segment_row):
    scores = jnp.einsum(
        "qhd,khd->hqk", query_block, key_row, preferred_element_type=jnp.float32
    ) * HEAD_DIM ** (-0.5)
    same = segment_block[:, None] == segment_row[None, :]
    return jnp.where(same[None], scores, negative)


def attend(query, keys, values, segment_ids, width):
    rows_dev, length = segment_ids.shape
    per_row = length // width
    flat_segments = segment_ids.reshape(-1)

    def one_block(block):
        row_index = block // per_row
        query_block = lax.dynamic_slice_in_dim(query, block * width, width, 0)
        segment_block = lax.dynamic_slice_in_dim(flat_segments, block * width, width, 0)
        scores = block_scores(query_block, keys[row_index], segment_block, segment_ids[row_index])
        peak_score = jnp.max(scores, -1, keepdims=True)
        weights = jnp.exp(scores - peak_score)
        totals = jnp.sum(weights, -1, keepdims=True)
        probs = (weights / totals).astype(jnp.bfloat16)
        output = jnp.einsum(
            "hqk,khd->qhd", probs, values[row_index], preferred_element_type=jnp.float32
        )
        return (output, (peak_score + jnp.log(totals))[..., 0])

    outputs, log_totals = lax.map(one_block, jnp.arange(rows_dev * per_row, dtype=jnp.int32))
    return (outputs.reshape((rows_dev * length,) + outputs.shape[2:]), log_totals)


def attend_back(query, keys, values, segment_ids, log_totals, grad_out, width):
    rows_dev, length = segment_ids.shape
    per_row = length // width
    flat_segments = segment_ids.reshape(-1)
    factor = HEAD_DIM ** (-0.5)

    def one_block(carry, block):
        grad_keys, grad_values = carry
        row_index = block // per_row
        query_block = lax.dynamic_slice_in_dim(query, block * width, width, 0)
        segment_block = lax.dynamic_slice_in_dim(flat_segments, block * width, width, 0)
        grad_block = lax.dynamic_slice_in_dim(grad_out, block * width, width, 0)
        scores = block_scores(query_block, keys[row_index], segment_block, segment_ids[row_index])
        probs = jnp.exp(scores - log_totals[block][..., None])
        grad_probs = jnp.einsum(
            "qhd,khd->hqk", grad_block, values[row_index], preferred_element_type=jnp.float32
        )
        inner = jnp.sum(probs * grad_probs, -1, keepdims=True)
        grad_scores = (probs * (grad_probs - inner)).astype(jnp.bfloat16)
        grad_query = (
            jnp.einsum(
                "hqk,khd->qhd", grad_scores, keys[row_index], preferred_element_type=jnp.float32
            )
            * factor
        )
        key_term = (
            jnp.einsum("hqk,qhd->khd", grad_scores, query_block, preferred_element_type=jnp.float32)
            * factor
        )
        value_term = jnp.einsum(
            "hqk,qhd->khd",
            probs.astype(jnp.bfloat16),
            grad_block,
            preferred_element_type=jnp.float32,
        )
        return (
            (grad_keys.at[row_index].add(key_term), grad_values.at[row_index].add(value_term)),
            grad_query,
        )

    zeros = jnp.zeros(keys.shape, jnp.float32)
    (grad_keys, grad_values), grad_query = lax.scan(
        one_block, (zeros, zeros), jnp.arange(rows_dev * per_row, dtype=jnp.int32)
    )
    return (grad_query.reshape((rows_dev * length,) + grad_query.shape[2:]), grad_keys, grad_values)


def adam_update(weight, grad, first, second, rate):
    first = 0.5 * first + 0.5 * grad
    second = 0.5 * second + 0.5 * grad * grad
    correction = 1.0 - 0.5**step_number
    weight = weight - rate * (
        first / correction / (jnp.sqrt(second / correction) + 1e-08) + 0.01 * weight
    )
    return (weight, first, second)


def local(
    token_ids,
    segment_ids,
    row_of,
    query_count,
    table,
    qkv_weight,
    out_weight,
    gate_up_weight,
    down_weight,
    gains,
    table_m,
    qkv_m,
    out_m,
    gate_up_m,
    down_m,
    gains_m,
    table_v,
    qkv_v,
    out_v,
    gate_up_v,
    down_v,
    gains_v,
):
    local_width = table.shape[1] // lax.axis_size("mp")
    column = lax.axis_index("mp") * local_width
    table_cols = lax.dynamic_slice_in_dim(table, column, local_width, 1)
    low_table, w_qkv, w_out, w_gu, w_down, gain_low = (
        lax.all_gather(table_cols.astype(jnp.bfloat16), "batch", axis=0, tiled=True),
        lax.all_gather(qkv_weight.astype(jnp.bfloat16), "batch", axis=0, tiled=True),
        lax.all_gather(out_weight.astype(jnp.bfloat16), "batch", axis=1, tiled=True),
        lax.all_gather(gate_up_weight.astype(jnp.bfloat16), "batch", axis=0, tiled=True),
        lax.all_gather(down_weight.astype(jnp.bfloat16), "batch", axis=1, tiled=True),
        lax.all_gather(gains.astype(jnp.bfloat16), "batch", axis=1, tiled=True),
    )
    gain = gain_low.astype(jnp.float32)
    rows_dev, length = token_ids.shape
    tokens = rows_dev * length
    width = min(512, length)
    heads_local = w_qkv.shape[2] // HEAD_DIM
    ff_local = w_gu.shape[2]
    table_rows = row_of[token_ids.reshape(-1)]
    x_zero = lax.all_gather(low_table[table_rows], "mp", axis=1, tiled=True)
    places = jax.vmap(partial(positions, segment_count=SEGS))(segment_ids).reshape(-1)
    qkv = jnp.dot(x_zero, w_qkv.reshape(D, -1), preferred_element_type=jnp.float32).reshape(
        tokens, 3, heads_local, HEAD_DIM
    )
    query = rotate(qkv[:, 0], places).astype(jnp.bfloat16)
    keys = (
        rotate(qkv[:, 1], places)
        .astype(jnp.bfloat16)
        .reshape(rows_dev, length, heads_local, HEAD_DIM)
    )
    values = qkv[:, 2].astype(jnp.bfloat16).reshape(rows_dev, length, heads_local, HEAD_DIM)
    attended, log_totals = attend(query, keys, values, segment_ids, width)
    attended_low = attended.reshape(tokens, -1).astype(jnp.bfloat16)
    attn_term = jnp.dot(attended_low, w_out, preferred_element_type=jnp.float32)
    attn = lax.psum(attn_term, "mp")
    hidden_one, first_back = jax.vjp(layer_norm, x_zero.astype(jnp.float32) + attn, gain[0])
    hidden_low = hidden_one.astype(jnp.bfloat16)
    gate_up = jnp.dot(hidden_low, w_gu.reshape(D, -1), preferred_element_type=jnp.float32).reshape(
        tokens, 2, ff_local
    )
    active, swiglu_back = jax.vjp(swiglu, gate_up)
    active_low = active.astype(jnp.bfloat16)
    mlp = lax.psum(jnp.dot(active_low, w_down, preferred_element_type=jnp.float32), "mp")
    hidden_two, second_back = jax.vjp(layer_norm, hidden_one + mlp, gain[1])
    embed, pool_back = jax.vjp(lambda hidden: pool_rows(hidden, segment_ids), hidden_two)
    batch_index = lax.axis_index("batch")
    half_count = lax.axis_size("batch") // 2
    texts = embed.shape[0]
    queries_all = half_count * texts
    everyone = lax.all_gather(embed, "batch", axis=0, tiled=True)
    question_vectors = everyone[:queries_all]
    passage_vectors = everyone[queries_all:]
    limit = query_count[0].astype(jnp.float32)
    labels = jnp.arange(queries_all, dtype=jnp.int32)
    weight_rows = (labels < query_count[0]).astype(jnp.float32) / limit
    affinity_scores = (
        jnp.dot(question_vectors, passage_vectors.T, precision=peak_affinity) / sharpness_divisor
    )
    target = (labels[:, None] == labels[None, :]).astype(jnp.float32)
    loss_value = jnp.sum(
        weight_rows
        * (jax.nn.logsumexp(affinity_scores, -1) - jnp.sum(affinity_scores * target, -1))
    )
    affinity_derivative = (jax.nn.softmax(affinity_scores, -1) - target) * weight_rows[:, None]
    grad_all = jnp.concatenate(
        [
            jnp.dot(affinity_derivative, passage_vectors, precision=peak_affinity)
            / sharpness_divisor,
            jnp.dot(affinity_derivative.T, question_vectors, precision=peak_affinity)
            / sharpness_divisor,
        ],
        0,
    )
    grad_embed = lax.dynamic_slice_in_dim(grad_all, batch_index * texts, texts, 0)
    (grad_two,) = pool_back(grad_embed)
    grad_second, grad_gain_two = second_back(grad_two)
    grad_mlp_low = grad_second.astype(jnp.bfloat16)
    grad_active = contract(grad_mlp_low, w_down, 1, 1)
    grad_down = contract(active_low, grad_mlp_low, 0, 0)
    (grad_gate_up,) = swiglu_back(grad_active)
    grad_gu_low = grad_gate_up.reshape(tokens, -1).astype(jnp.bfloat16)
    back_term = contract(grad_gu_low, w_gu.reshape(D, -1), 1, 1)
    grad_one = grad_second + lax.psum(back_term, "mp")
    grad_first, grad_gain_one = first_back(grad_one)
    grad_gu = contract(hidden_low, grad_gu_low, 0, 0)
    grad_attn_low = grad_first.astype(jnp.bfloat16)
    grad_attended = contract(grad_attn_low, w_out, 1, 1).astype(jnp.bfloat16)
    grad_out = contract(attended_low, grad_attn_low, 0, 0)
    grad_query, grad_keys, grad_values = attend_back(
        query,
        keys,
        values,
        segment_ids,
        log_totals,
        grad_attended.reshape(tokens, heads_local, HEAD_DIM),
        width,
    )
    _, rotate_back = jax.vjp(lambda inputs: rotate(inputs, places), qkv[:, 0])
    (grad_query_raw,) = rotate_back(grad_query)
    (grad_key_raw,) = rotate_back(grad_keys.reshape(tokens, heads_local, HEAD_DIM))
    grad_qkv_low = (
        jnp.stack(
            [grad_query_raw, grad_key_raw, grad_values.reshape(tokens, heads_local, HEAD_DIM)], 1
        )
        .reshape(tokens, -1)
        .astype(jnp.bfloat16)
    )
    grad_zero = grad_first + lax.psum(contract(grad_qkv_low, w_qkv.reshape(D, -1), 1, 1), "mp")
    grad_qkv = contract(x_zero, grad_qkv_low, 0, 0)
    grad_table = (
        jnp.zeros((low_table.shape[0], local_width), jnp.float32)
        .at[table_rows]
        .add(lax.dynamic_slice_in_dim(grad_zero, column, local_width, 1))
    )
    grad_gains = jnp.stack([grad_gain_one, grad_gain_two], 0)
    reduced = (
        lax.psum_scatter(grad_table, "batch", scatter_dimension=0, tiled=True),
        lax.psum_scatter(grad_qkv.reshape(D, 3, -1), "batch", scatter_dimension=0, tiled=True),
        lax.psum_scatter(grad_out, "batch", scatter_dimension=1, tiled=True),
        lax.psum_scatter(grad_gu.reshape(D, 2, -1), "batch", scatter_dimension=0, tiled=True),
        lax.psum_scatter(grad_down, "batch", scatter_dimension=1, tiled=True),
        lax.psum_scatter(grad_gains, "batch", scatter_dimension=1, tiled=True),
    )
    squares = sum((jnp.sum(part * part) for part in reduced[:5])) + jnp.sum(
        reduced[5] * reduced[5]
    ) / lax.axis_size("mp")
    table_full = lax.all_gather(reduced[0], "mp", axis=1, tiled=True)
    total_squares = lax.psum(squares, ("batch", "mp"))
    grad_norm = jnp.sqrt(total_squares)
    scale = clip_limit / jnp.maximum(grad_norm, clip_limit)
    olds = (table, qkv_weight, out_weight, gate_up_weight, down_weight, gains)
    grads_all = (table_full,) + tuple(reduced[1:])
    firsts = (table_m, qkv_m, out_m, gate_up_m, down_m, gains_m)
    seconds = (table_v, qkv_v, out_v, gate_up_v, down_v, gains_v)
    updated = [
        adam_update(weight_old, grad_part * scale, first_old, second_old, rate)
        for weight_old, grad_part, first_old, second_old, rate in zip(
            olds, grads_all, firsts, seconds, rates
        )
    ]
    clipped_table = table_full * scale
    loss = loss_value.reshape(1)
    return (
        loss,
        grad_norm.reshape(1),
        updated[0][0],
        updated[1][0],
        updated[2][0],
        updated[3][0],
        updated[4][0],
        updated[5][0],
        clipped_table,
        updated[1][1],
        updated[2][1],
        updated[3][1],
        updated[4][1],
        updated[5][1],
        updated[0][2],
        updated[1][2],
        updated[2][2],
        updated[3][2],
        updated[4][2],
        updated[5][2],
    )


def solution(mesh):
    placed = (
        P("batch", None),
        P("batch", None),
        P(),
        P(),
        P("batch", None),
        P("batch", None, "mp"),
        P("mp", "batch"),
        P("batch", None, "mp"),
        P("mp", "batch"),
        P(None, "batch"),
        P("batch", None),
        P("batch", None, "mp"),
        P("mp", "batch"),
        P("batch", None, "mp"),
        P("mp", "batch"),
        P(None, "batch"),
        P("batch", None),
        P("batch", None, "mp"),
        P("mp", "batch"),
        P("batch", None, "mp"),
        P("mp", "batch"),
        P(None, "batch"),
    )
    return jax.shard_map(
        local,
        mesh=mesh,
        in_specs=placed,
        out_specs=(
            P(),
            P(),
            P("batch", None),
            P("batch", None, "mp"),
            P("mp", "batch"),
            P("batch", None, "mp"),
            P("mp", "batch"),
            P(None, "batch"),
            P("batch", None),
            P("batch", None, "mp"),
            P("mp", "batch"),
            P("batch", None, "mp"),
            P("mp", "batch"),
            P(None, "batch"),
            P("batch", None),
            P("batch", None, "mp"),
            P("mp", "batch"),
            P("batch", None, "mp"),
            P("mp", "batch"),
            P(None, "batch"),
        ),
        check_vma=False,
    )
```

profile of v0, /device:TPU:0, one launch (start us, length us, event | category | flops | bytes accessed | tf_op | source)
XLA Modules:
  0.0 1895.6 jit_solution(3074774490312549609)
XLA Ops:
  7.3 12.4 copy.141
  22.9 8.4 gather_fusion
  31.4 63.1 %all-gather.17.cloned.1.call-done = bf16[8,3816,192]{1,2,0:T(8,128)(2,1)} async-done(((bf16[1,3816,192]{1,2,0:T(8,128)(2,1)}), bf16[8,3816,192]{1,2,0:T(8,128)(2,1)}) %all-gather.17.cloned.1.call-update) | async-done | bytes 11722768 | tf_op jit(solution)/shard_map/all_gather | solution.py:181
  94.5 18.1 copy.142
  112.6 11.2 gather_fusion.1
  126.6 13.2 all_gather.29
  141.9 9.2 all_gather.30
  151.9 23.6 %all-gather.15.cloned.1.call-done = bf16[1536,768]{0,1:T(8,128)(2,1)} async-done(((bf16[1536,192]{0,1:T(8,128)(2,1)}), bf16[1536,768]{0,1:T(8,128)(2,1)}) %all-gather.15.cloned.1.call-update) | async-done | bytes 2359312 | tf_op jit(solution)/shard_map/all_gather | solution.py:195
  179.8 33.9 %while.31 = (s32[]{:T(128)}, bf16[3,512,3,64]{1,3,2,0:T(8,128)(2,1)}, f32[3,3,512]{2,1,0:T(4,128)S(1)}, s32[3]{0:T(128)S(1)}, s32[1536]{0:T(1024)S(1)}, /*index=...) while((s32[]{:T(128)}, ...), condition=%wide.region_6.7_spmd, body=%wide.region_3.6_spmd.sunk | while | flops 633076224 | bytes 38029568 | solution.py:92
  219.3 8.9 all-gather.2
  228.3 4.3 copy.151
  232.6 156.8 %all-reduce.11.cloned.1.call-done = f32[1536,768]{0,1:T(8,128)} async-done(((f32[1536,768]{0,1:T(8,128)}), f32[1536,768]{0,1:T(8,128)}) %all-reduce.11.cloned.1.call-update) | async-done | bytes 4718608 | tf_op jit(solution)/shard_map/psum | solution.py:210
  407.1 7.7 all-gather.11.cloned.1.call-done
  414.8 6.2 fusion.123
  421.9 171.2 %all-reduce.13.cloned.1.call-done = f32[1536,768]{0,1:T(8,128)} async-done(((f32[1536,768]{0,1:T(8,128)}), f32[1536,768]{0,1:T(8,128)}) %all-reduce.13.cloned.1.call-update) | async-done | bytes 4718608 | tf_op jit(solution)/shard_map/psum | solution.py:218
  593.1 4.7 fusion.118
  601.2 9.5 all_gather.34
  617.9 5.3 multiply_bitcast_fusion
  625.3 7.9 convolution_bitcast_fusion
  633.7 169.7 %all-reduce.15.cloned.1.call-done = f32[1536,768]{0,1:T(8,128)} async-done(((f32[1536,768]{0,1:T(8,128)}), f32[1536,768]{0,1:T(8,128)}) %all-reduce.15.cloned.1.call-update) | async-done | bytes 4718608 | tf_op jit(solution)/shard_map/psum | solution.py:258
  803.4 6.2 multiply_reduce_fusion.2
  809.6 4.5 multiply_reduce_fusion.1
  821.4 161.7 %while.32 = (s32[]{:T(128)}, f32[1,1536,3,64]{1,3,2,0:T(8,128)}, f32[1,1536,3,64]{1,3,2,0:T(8,128)S(1)}, f32[3,512,3,64]{1,0,3,2:T(4,128)}, s32[3]{0:T(128)S(1)}...) while((s32[]{:T(128)}, f32[1,1536,3,64]{1,3,2,0:T(8,128)}, ...), condition=%wide.region_29.30_spmd.clone, body=%wide.region_26.29_spmd.clone.sunk | while | flops 1534130688 | bytes 86367704 | solution.py:137
  822.6 6.1 fusion.167
  831.3 8.1 multiply_reduce_fusion.16
  839.3 9.4 multiply_convert_fusion.4
  853.0 8.6 dynamic_update_slice.22
  864.3 5.1 fusion.168
  869.4 5.6 fusion.169
  876.3 6.1 fusion.167
  885.0 8.1 multiply_reduce_fusion.16
  893.0 9.4 multiply_convert_fusion.4
  906.7 8.6 dynamic_update_slice.22
  918.0 5.4 fusion.168
  923.4 5.6 fusion.169
  930.4 6.1 fusion.167
  939.0 8.1 multiply_reduce_fusion.16
  947.1 9.4 multiply_convert_fusion.4
  960.7 8.6 dynamic_update_slice.22
  972.1 5.4 fusion.168
  977.5 5.6 fusion.169
  988.7 4.2 fusion.121
  993.0 171.1 %all-reduce.17.cloned.1.call-done = f32[1536,768]{0,1:T(8,128)} async-done(((f32[1536,768]{0,1:T(8,128)}), f32[1536,768]{0,1:T(8,128)}) %all-reduce.17.cloned.1.call-update) | async-done | bytes 4718608 | tf_op jit(solution)/shard_map/psum | solution.py:283
  1166.3 21.2 %scatter_custom_fusion = f32[30528,192]{1,0:T(8,128)} fusion(s32[1536]{0:T(1024)} %copy-done.49, f32[1536,192]{1,0:T(8,128)S(1)} %copy.157, f32[]{:T(128)} %constant.228.clone.1), kind=kCustom, calls=%fused_computation.51 | custom fusion | flops 294912 | bytes 23446016 | tf_op jit(solution)/shard_map/scatter-add | solution.py:288
  1189.1 5.8 fusion.74
  1196.3 5.3 convolution_bitcast_fusion.1
  1201.7 15.3 fusion.50
  1219.2 5.4 fusion.63
  1224.7 151.4 %reduce-scatter.11.cloned.1.call-done = f32[3816,192]{1,0:T(8,128)} async-done(((f32[30528,192]{1,0:T(8,128)}), f32[3816,192]{1,0:T(8,128)}) %reduce-scatter.11.cloned.1.call-update) | async-done | bytes 2930704 | tf_op jit(solution)/shard_map/reduce_scatter | solution.py:292
  1376.1 5.1 copy.159
  1381.2 12.6 copy.160
  1393.8 28.0 %reduce-scatter.17.cloned.1.call-done = f32[768,96]{0,1:T(8,128)} async-done(((f32[768,768]{0,1:T(8,128)}), f32[768,96]{0,1:T(8,128)}) %reduce-scatter.17.cloned.1.call-update) | async-done | bytes 294928 | tf_op jit(solution)/shard_map/reduce_scatter | solution.py:296
  1423.5 36.1 %reduce-scatter.21.cloned.1.call-done = f32[96,2]{1,0:T(8,128)} async-done(((f32[768,2]{1,0:T(8,128)}), f32[96,2]{1,0:T(8,128)}) %reduce-scatter.21.cloned.1.call-update) | async-done | bytes 784
  1461.8 36.2 %reduce-scatter.19.cloned.1.call-done = f32[96,192]{1,0:T(8,128)} async-done(((f32[768,192]{1,0:T(8,128)}), f32[96,192]{1,0:T(8,128)}) %reduce-scatter.19.cloned.1.call-update) | async-done | bytes 73744
  1499.6 56.7 %reduce-scatter.15.cloned.1.call-done = f32[96,2,768]{2,0,1:T(8,128)} async-done(((f32[768,2,768]{2,0,1:T(8,128)}), f32[96,2,768]{2,0,1:T(8,128)}) %reduce-scatter.15.cloned.1.call-update) | async-done | bytes 589840 | tf_op jit(solution)/shard_map/reduce_scatter | solution.py:295
  1558.1 44.5 %reduce-scatter.13.cloned.1.call-done = f32[96,3,192]{2,0,1:T(8,128)} async-done(((f32[768,3,192]{2,0,1:T(8,128)}), f32[96,3,192]{2,0,1:T(8,128)}) %reduce-scatter.13.cloned.1.call-update) | async-done | bytes 221200 | tf_op jit(solution)/shard_map/reduce_scatter | solution.py:293
  1611.3 13.3 copy.158
  1624.7 53.5 %psum.39 = f32[]{:T(128)} all-reduce(f32[]{:T(128)S(6)} %add.324), channel_id=1, replica_groups=mesh['batch'=8,'mp'=4] {'batch','mp'}, use_global_device_ids=true, to_apply=%region_46.47 | all-reduce | flops 1 | bytes 8 | tf_op jit(solution)/shard_map/psum | solution.py:303
  1687.7 123.4 %all-gather.13.cloned.1.call-done = f32[3816,768]{0,1:T(8,128)} async-done(((f32[3816,192]{0,1:T(8,128)}), f32[3816,768]{0,1:T(8,128)}) %all-gather.13.cloned.1.call-update) | async-done | bytes 11722768 | tf_op jit(solution)/shard_map/all_gather | solution.py:302
  1811.0 17.3 fusion.46
  1828.4 12.3 copy.169
  1840.7 22.2 %fusion.45 = f32[3816,768]{0,1:T(8,128)} fusion(f32[3816,768]{0,1:T(8,128)} %copy.141, f32[3816,768]{0,1:T(8,128)} %get-tuple-element.440, f32[3816,768]{0,1:T(8,128)} %copy.158, f32[3816,768]{0,1:T(8,128)} %copy.160), kind=kLoop, calls=%fused_computation.57 | loop fusion | flops 41029632 | bytes 58613760 | tf_op jit(solution)/shard_map/sub | solution.py:147
  1862.9 12.3 copy.167
  1875.3 12.4 copy.171
  (315 shorter events, 141.3 us)
Async XLA Ops:
  7.2 15.7 copy-start
  7.2 87.3 %all-gather.17.cloned.1.call-start = ((), (), s32[]{:S(2)}) async-start(), calls=%async_computation.18 | async-start | bytes 13271040 | tf_op jit(solution)/shard_map/all_gather | solution.py:181
  7.3 15.6 copy-start.52
  22.8 152.7 %all-gather.15.cloned.1.call-start = ((), (), s32[]{:S(2)}) async-start(), calls=%async_computation.17 | async-start | bytes 2949120 | tf_op jit(solution)/shard_map/all_gather | solution.py:195
  31.4 81.2 %copy-start.49 = (s32[1536]{0:T(1024)}, s32[1536]{0:T(1024)S(1)}, u32[]{:S(2)}) copy-start(s32[1536]{0:T(1024)S(1)} %fusion.104) | copy-start | bytes 18436
  112.5 12.4 copy-start.12
  112.5 13.2 copy-start.30
  112.5 13.9 copy-start.25
  123.7 18.1 copy-start.35
  124.8 103.5 %all-gather.9.cloned.1.call-start = ((), (), s32[]{:S(2)}) async-start(), calls=%async_computation.7 | async-start | bytes 2654208 | tf_op jit(solution)/shard_map/all_gather | solution.py:184
  125.7 263.7 %all-reduce.11.cloned.1.call-start = ((), (), s32[]{:S(2)}) async-start(), calls=%async_computation.6 | async-start | bytes 9437184 | tf_op jit(solution)/shard_map/psum | solution.py:210
  151.1 64.4 %copy-start.10 = (bf16[192,768]{0,1:T(8,128)(2,1)}, bf16[192,768]{0,1:T(8,128)(2,1)S(1)}, u32[]{:S(2)}) copy-start(bf16[192,768]{0,1:T(8,128)(2,1)S(1)} %all_gather.30) | copy-start | bytes 884740
  151.8 27.5 %copy-start.19 = (f32[1536,32]{0,1:T(8,128)}, f32[1536,32]{0,1:T(8,128)S(1)}, u32[]{:S(2)}) copy-start(f32[1536,32]{0,1:T(8,128)S(1)} %get-tuple-element.486) | copy-start | bytes 589828
  151.9 27.5 %copy-start.21 = (f32[1536,32]{0,1:T(8,128)}, f32[1536,32]{0,1:T(8,128)S(1)}, u32[]{:S(2)}) copy-start(f32[1536,32]{0,1:T(8,128)S(1)} %get-tuple-element.487) | copy-start | bytes 589828
  218.5 196.3 %all-gather.11.cloned.1.call-start = ((), (), s32[]{:S(2)}) async-start(), calls=%async_computation.8 | async-start | bytes 1327104 | tf_op jit(solution)/shard_map/all_gather | solution.py:185
  219.2 373.9 %all-reduce.13.cloned.1.call-start = ((), (), s32[]{:S(2)}) async-start(), calls=%async_computation.9 | async-start | bytes 9437184 | tf_op jit(solution)/shard_map/psum | solution.py:218
  228.3 585.8 %copy-start.45 = (f32[768]{0:T(1024)}, f32[768]{0:T(1024)S(1)}, u32[]{:S(2)}) copy-start(f32[768]{0:T(1024)S(1)} %get-tuple-element.396) | copy-start | bytes 9220
  393.4 7.4 copy-start.2
  393.4 420.7 %copy-start.41 = (f32[1536]{0:T(1024)}, f32[1536]{0:T(1024)S(1)}, u32[]{:S(2)}) copy-start(f32[1536]{0:T(1024)S(1)} %broadcast_multiply_fusion.3) | copy-start | bytes 18436
  393.9 420.1 %copy-start.43 = (f32[1536]{0:T(1024)}, f32[1536]{0:T(1024)S(1)}, u32[]{:S(2)}) copy-start(f32[1536]{0:T(1024)S(1)} %fusion.101) | copy-start | bytes 18436
  421.0 382.4 %all-reduce.15.cloned.1.call-start = ((), (), s32[]{:S(2)}) async-start(), calls=%async_computation.10 | async-start | bytes 9437184 | tf_op jit(solution)/shard_map/psum | solution.py:258
  612.3 5.2 slice-start.1
  617.5 5.6 copy-start.6
  617.5 185.9 %copy-start.47 = (f32[1536]{0:T(1024)}, f32[1536]{0:T(1024)S(1)}, u32[]{:S(2)}) copy-start(f32[1536]{0:T(1024)S(1)} %negate_multiply_fusion.1) | copy-start | bytes 18436
  617.9 7.5 copy-start.16
  633.2 530.8 %all-reduce.17.cloned.1.call-start = ((), (), s32[]{:S(2)}) async-start(), calls=%async_computation.11 | async-start | bytes 9437184 | tf_op jit(solution)/shard_map/psum | solution.py:283
  814.1 5.8 copy-start.11
  821.4 163.9 %copy-start.20 = (f32[1536,32]{0,1:T(8,128)S(1)}, f32[1536,32]{0,1:T(8,128)}, u32[]{:S(2)}) copy-start(f32[1536,32]{0,1:T(8,128)} %copy-done.19) | copy-start | bytes 589828
  821.4 7.3 copy-start.4
  869.4 5.6 copy-start.5
  875.0 7.5 copy-start.4
  923.4 5.6 copy-start.5
  929.0 7.5 copy-start.4
  977.5 5.6 copy-start.5
  992.9 383.2 %reduce-scatter.11.cloned.1.call-start = ((), (), s32[]{:S(2)}) async-start(), calls=%async_computation.12 | async-start | bytes 35168256 | tf_op jit(solution)/shard_map/reduce_scatter | solution.py:292
  1187.5 7.5 copy-start.50
  1187.5 7.5 copy-start.51
  1187.5 8.8 copy-start.9
  1187.5 234.4 %reduce-scatter.17.cloned.1.call-start = ((), (), s32[]{:S(2)}) async-start(), calls=%async_computation.15 | async-start | bytes 2654208 | tf_op jit(solution)/shard_map/reduce_scatter | solution.py:296
  1194.9 6.8 copy-start.42
  1194.9 6.8 copy-start.44
  1194.9 6.8 copy-start.46
  1194.9 264.7 %reduce-scatter.21.cloned.1.call-start = ((), (), s32[]{:S(2)}) async-start(), calls=%async_computation.20 | async-start | bytes 442368
  1196.0 302.0 %reduce-scatter.19.cloned.1.call-start = ((), (), s32[]{:S(2)}) async-start(), calls=%async_computation.19 | async-start | bytes 884736
  1201.7 354.7 %reduce-scatter.15.cloned.1.call-start = ((), (), s32[]{:S(2)}) async-start(), calls=%async_computation.14 | async-start | bytes 5308416 | tf_op jit(solution)/shard_map/reduce_scatter | solution.py:295
  1217.1 385.6 %reduce-scatter.13.cloned.1.call-start = ((), (), s32[]{:S(2)}) async-start(), calls=%async_computation.13 | async-start | bytes 2654208 | tf_op jit(solution)/shard_map/reduce_scatter | solution.py:293
  1224.7 586.4 %all-gather.13.cloned.1.call-start = ((), (), s32[]{:S(2)}) async-start(), calls=%async_computation.16 | async-start | bytes 14745600 | tf_op jit(solution)/shard_map/all_gather | solution.py:302
  1611.3 67.6 %copy-start.13 = (f32[96,2,768]{2,1,0:T(2,128)S(1)}, f32[96,2,768]{2,1,0:T(2,128)}, u32[]{:S(2)}) copy-start(f32[96,2,768]{2,1,0:T(2,128)} %param.37) | copy-start | bytes 1769476
  1611.3 67.6 %copy-start.14 = (f32[96,2,768]{2,0,1:T(8,128)S(1)}, f32[96,2,768]{2,0,1:T(8,128)}, u32[]{:S(2)}) copy-start(f32[96,2,768]{2,0,1:T(8,128)} %reduce-scatter.15.cloned.1.call-done) | copy-start | bytes 1769476
  1611.3 67.6 %copy-start.31 = (f32[96,2,768]{2,1,0:T(2,128)S(1)}, f32[96,2,768]{2,1,0:T(2,128)}, u32[]{:S(2)}) copy-start(f32[96,2,768]{2,1,0:T(2,128)} %param.43) | copy-start | bytes 1769476
  1611.3 67.6 %copy-start.32 = (f32[96,2,768]{2,1,0:T(2,128)S(1)}, f32[96,2,768]{2,1,0:T(2,128)}, u32[]{:S(2)}) copy-start(f32[96,2,768]{2,1,0:T(2,128)} %param.49) | copy-start | bytes 1769476
  1624.6 58.6 %copy-start.54 = (f32[2,96]{1,0:T(2,128)S(1)}, f32[2,96]{1,0:T(2,128)}, u32[]{:S(2)}) copy-start(f32[2,96]{1,0:T(2,128)} %param.39) | copy-start | bytes 2308
  1624.6 58.6 %copy-start.55 = (f32[2,96]{1,0:T(2,128)S(1)}, f32[2,96]{1,0:T(2,128)}, u32[]{:S(2)}) copy-start(f32[2,96]{1,0:T(2,128)} %param.45) | copy-start | bytes 2308
  1624.6 58.6 %copy-start.56 = (f32[2,96]{1,0:T(2,128)S(1)}, f32[2,96]{1,0:T(2,128)}, u32[]{:S(2)}) copy-start(f32[2,96]{1,0:T(2,128)} %param.51) | copy-start | bytes 2308
  1624.6 59.2 %copy-start.36 = (f32[192,96]{1,0:T(8,128)S(1)}, f32[192,96]{1,0:T(8,128)}, u32[]{:S(2)}) copy-start(f32[192,96]{1,0:T(8,128)} %param.36) | copy-start | bytes 221188
  1624.6 60.9 %copy-start.24 = (f32[768,96]{0,1:T(8,128)S(1)}, f32[768,96]{0,1:T(8,128)}, u32[]{:S(2)}) copy-start(f32[768,96]{0,1:T(8,128)} %param.38) | copy-start | bytes 884740
  1624.6 60.9 %copy-start.27 = (f32[768,96]{0,1:T(8,128)S(1)}, f32[768,96]{0,1:T(8,128)}, u32[]{:S(2)}) copy-start(f32[768,96]{0,1:T(8,128)} %reduce-scatter.17.cloned.1.call-done) | copy-start | bytes 884740
  1624.6 60.9 %copy-start.37 = (f32[768,96]{0,1:T(8,128)S(1)}, f32[768,96]{0,1:T(8,128)}, u32[]{:S(2)}) copy-start(f32[768,96]{0,1:T(8,128)} %param.44) | copy-start | bytes 884740
  1678.9 6.6 copy-start.38
  1678.9 7.7 copy-start.26
  1678.9 7.7 copy-start.28
  1678.9 7.7 copy-start.39
  1678.9 7.7 copy-start.40
  1875.3 12.4 copy-start.1
  (21 other events, 46.0 us)
Sparse Core Ops, SparseCore 0:
  22.9 71.4 all-gather.16
  125.0 50.4 all-gather.14
  178.0 27.8 all-gather.8
  218.6 170.7 all-reduce.10
  391.7 23.0 all-gather.10
  421.1 171.9 all-reduce.12
  633.3 170.0 all-reduce.14
  993.0 170.9 all-reduce.16
  1187.6 188.4 reduce-scatter.10
  1379.3 42.5 reduce-scatter.16
  1425.8 33.7 reduce-scatter.20
  1463.0 34.9 reduce-scatter.18
  1502.4 53.8 reduce-scatter.14
  1560.1 42.5 reduce-scatter.12
  1604.7 206.2 all-gather.12
where the time goes:
time: 1900 us
  waiting for transfers between devices  1240 us (65%)
  local copies, waits for them, and re-layouts  191 us (10%)
  matrix products  179 us (9%)
  other arithmetic  153 us (8%)
  blocking collectives  94.2 us (5%)
  between operations  21.7 us (1%)
    psum x1, waiting for transfers between devices, local(): lax.psum(jnp.dot(active_low, w_down, preferred_element_type=jnp.float32),...  171 us
    psum x1, waiting for transfers between devices, local(): lax.psum(contract(grad_qkv_low, w_qkv.reshape(D, -1), 1, 1), 'mp')  171 us
    psum x1, waiting for transfers between devices, local(): grad_one = grad_second + lax.psum(back_term, 'mp')  170 us
    psum x1, waiting for transfers between devices, local(): attn = lax.psum(attn_term, 'mp')  157 us
    reduce_scatter x1, waiting for transfers between devices, local(): lax.psum_scatter(grad_table, 'batch', scatter_dimension=0, tiled=True)  151 us
    all_gather x1, waiting for transfers between devices, local(): table_full = lax.all_gather(reduced[0], 'mp', axis=1, tiled=True)  123 us
    unnamed x132, local copies, waits for them, and re-layouts  102 us
    unnamed x17, waiting for transfers between devices  72.6 us
  transfers between devices with their start and end apart: 15, of which 14 were waited for; matrix products, arithmetic and copies ran while one was open for 8% of the time, Pallas kernels for 0%

commit v1 on v0

--- a/solution.py
+++ b/solution.py
@@ -207,7 +207,11 @@
     attended, log_totals = attend(query, keys, values, segment_ids, width)
     attended_low = attended.reshape(tokens, -1).astype(jnp.bfloat16)
     attn_term = jnp.dot(attended_low, w_out, preferred_element_type=jnp.float32)
-    attn = lax.psum(attn_term, "mp")
+
+    def track_slots_for(local_values):
+        return jnp.sum(lax.all_gather(local_values, "mp"), 0)
+
+    attn = track_slots_for(attn_term)
     hidden_one, first_back = jax.vjp(layer_norm, x_zero.astype(jnp.float32) + attn, gain[0])
     hidden_low = hidden_one.astype(jnp.bfloat16)
     gate_up = jnp.dot(hidden_low, w_gu.reshape(D, -1), preferred_element_type=jnp.float32).reshape(

time: 1900 us -> 2060 us (1.084)
  waiting for transfers between devices: 1240 us -> 1380 us
    all_gather x0 -> x1, waiting for transfers between devices: none -> 307 us  [track_slots_for(): return jnp.sum(lax.all_gather(local_values, 'mp'), 0)]
    psum x1 -> x0, waiting for transfers between devices: 157 us -> none  [local(): attn = lax.psum(attn_term, 'mp')]
  transfers between devices with their start and end apart: 15 -> 15, of which waited for: 14 -> 13; matrix products, arithmetic and copies ran while one was open for 8% -> 8% of each run, Pallas kernels for 0% -> 0%
where the time goes in v1:
time: 2060 us; the launch traced here: 2050 us
  waiting for transfers between devices  1380 us (67%)
  local copies, waits for them, and re-layouts  197 us (10%)
  matrix products  178 us (9%)
  other arithmetic  164 us (8%)
  blocking collectives  93.7 us (5%)
  between operations  21.6 us (1%)
    all_gather x1, waiting for transfers between devices, track_slots_for(): return jnp.sum(lax.all_gather(local_values, 'mp'), 0)  307 us
    psum x1, waiting for transfers between devices, local(): lax.psum(contract(grad_qkv_low, w_qkv.reshape(D, -1), 1, 1), 'mp')  171 us
    psum x1, waiting for transfers between devices, local(): grad_one = grad_second + lax.psum(back_term, 'mp')  170 us
    psum x1, waiting for transfers between devices, local(): lax.psum(jnp.dot(active_low, w_down, preferred_element_type=jnp.float32),...  169 us
    reduce_scatter x1, waiting for transfers between devices, local(): lax.psum_scatter(grad_table, 'batch', scatter_dimension=0, tiled=True)  151 us
    all_gather x1, waiting for transfers between devices, local(): table_full = lax.all_gather(reduced[0], 'mp', axis=1, tiled=True)  123 us
    unnamed x132, local copies, waits for them, and re-layouts  102 us
    unnamed x17, waiting for transfers between devices  72.6 us
  transfers between devices with their start and end apart: 15, of which 13 were waited for; matrix products, arithmetic and copies ran while one was open for 8% of the time, Pallas kernels for 0%

profile of v1, /device:TPU:0, one launch (start us, length us, event | category | flops | bytes accessed | tf_op | source)
XLA Modules:
  0.0 2053.6 jit_solution(3973925150874206368)
XLA Ops:
  7.3 12.4 copy.139
  22.9 8.4 gather_fusion
  31.4 63.1 %all-gather.21.cloned.1.call-done = bf16[8,3816,192]{1,2,0:T(8,128)(2,1)} async-done(((bf16[1,3816,192]{1,2,0:T(8,128)(2,1)}), bf16[8,3816,192]{1,2,0:T(8,128)(2,1)}) %all-gather.21.cloned.1.call-update) | async-done | bytes 11722768 | tf_op jit(solution)/shard_map/all_gather | solution.py:181
  94.5 18.1 copy.140
  112.6 11.2 gather_fusion.1
  126.6 13.2 all_gather.35
  141.9 8.8 all_gather.36
  151.5 24.0 %all-gather.17.cloned.1.call-done = bf16[1536,768]{0,1:T(8,128)(2,1)} async-done(((bf16[1536,192]{0,1:T(8,128)(2,1)}), bf16[1536,768]{0,1:T(8,128)(2,1)}) %all-gather.17.cloned.1.call-update) | async-done | bytes 2359312 | tf_op jit(solution)/shard_map/all_gather | solution.py:195
  179.8 33.9 %while.31 = (s32[]{:T(128)}, bf16[3,512,3,64]{1,3,2,0:T(8,128)(2,1)}, f32[3,3,512]{2,1,0:T(4,128)S(1)}, s32[3]{0:T(128)S(1)}, s32[1536]{0:T(1024)S(1)}, /*index=...) while((s32[]{:T(128)}, ...), condition=%wide.region_6.7_spmd, body=%wide.region_3.6_spmd.sunk | while | flops 633076224 | bytes 38029568 | solution.py:92
  219.4 8.9 all-gather.3
  228.5 4.6 copy.149
  233.1 307.0 %all-gather.19.cloned.1.call-done = f32[6144,768]{1,0:T(8,128)} async-done(((f32[1536,768]{1,0:T(8,128)}), f32[6144,768]{1,0:T(8,128)}) %all-gather.19.cloned.1.call-update) | async-done | bytes 18874384 | tf_op jit(solution)/shard_map/all_gather | solution.py:212
  540.1 10.4 reduce_sum.285
  550.5 6.0 copy.146
  574.4 6.2 fusion.123
  581.9 169.5 %all-reduce.10.cloned.1.call-done = f32[1536,768]{0,1:T(8,128)} async-done(((f32[1536,768]{0,1:T(8,128)}), f32[1536,768]{0,1:T(8,128)}) %all-reduce.10.cloned.1.call-update) | async-done | bytes 4718608 | tf_op jit(solution)/shard_map/psum | solution.py:222
  751.4 4.7 fusion.118
  759.5 9.3 all_gather.42
  775.9 5.3 multiply_bitcast_fusion
  783.4 7.9 convolution_bitcast_fusion
  791.5 169.9 %all-reduce.12.cloned.1.call-done = f32[1536,768]{0,1:T(8,128)} async-done(((f32[1536,768]{0,1:T(8,128)}), f32[1536,768]{0,1:T(8,128)}) %all-reduce.12.cloned.1.call-update) | async-done | bytes 4718608 | tf_op jit(solution)/shard_map/psum | solution.py:262
  961.5 6.2 multiply_reduce_fusion.2
  967.6 4.5 multiply_reduce_fusion.1
  979.4 161.7 %while.32 = (s32[]{:T(128)}, f32[1,1536,3,64]{1,3,2,0:T(8,128)}, f32[1,1536,3,64]{1,3,2,0:T(8,128)S(1)}, f32[3,512,3,64]{1,0,3,2:T(4,128)}, s32[3]{0:T(128)S(1)}...) while((s32[]{:T(128)}, f32[1,1536,3,64]{1,3,2,0:T(8,128)}, ...), condition=%wide.region_29.30_spmd.clone, body=%wide.region_26.29_spmd.clone.sunk | while | flops 1534130688 | bytes 86367704 | solution.py:137
  980.7 6.1 fusion.167
  989.3 8.1 multiply_reduce_fusion.16
  997.4 9.4 multiply_convert_fusion.4
  1011.0 8.6 dynamic_update_slice.22
  1022.4 5.1 fusion.168
  1027.4 5.6 fusion.169
  1034.4 6.1 fusion.167
  1043.0 8.1 multiply_reduce_fusion.16
  1051.1 9.4 multiply_convert_fusion.4
  1064.7 8.6 dynamic_update_slice.22
  1076.1 5.4 fusion.168
  1081.5 5.6 fusion.169
  1088.4 6.1 fusion.167
  1097.1 8.1 multiply_reduce_fusion.16
  1105.2 9.4 multiply_convert_fusion.4
  1118.8 8.6 dynamic_update_slice.22
  1130.1 5.4 fusion.168
  1135.5 5.6 fusion.169
  1151.1 171.1 %all-reduce.14.cloned.1.call-done = f32[1536,768]{0,1:T(8,128)} async-done(((f32[1536,768]{0,1:T(8,128)}), f32[1536,768]{0,1:T(8,128)}) %all-reduce.14.cloned.1.call-update) | async-done | bytes 4718608 | tf_op jit(solution)/shard_map/psum | solution.py:287
  1324.4 21.2 %scatter_custom_fusion = f32[30528,192]{1,0:T(8,128)} fusion(s32[1536]{0:T(1024)} %copy-done.49, f32[1536,192]{1,0:T(8,128)S(1)} %copy.155, f32[]{:T(128)} %constant.228.clone.1), kind=kCustom, calls=%fused_computation.51 | custom fusion | flops 294912 | bytes 23446016 | tf_op jit(solution)/shard_map/scatter-add | solution.py:292
  1347.2 5.8 fusion.74
  1354.6 5.2 convolution_bitcast_fusion.1
  1359.9 15.4 fusion.50
  1377.7 5.1 fusion.63
  1382.8 151.4 %reduce-scatter.11.cloned.1.call-done = f32[3816,192]{1,0:T(8,128)} async-done(((f32[30528,192]{1,0:T(8,128)}), f32[3816,192]{1,0:T(8,128)}) %reduce-scatter.11.cloned.1.call-update) | async-done | bytes 2930704 | tf_op jit(solution)/shard_map/reduce_scatter | solution.py:296
  1534.2 5.1 copy.157
  1539.3 12.6 copy.158
  1551.9 28.0 %reduce-scatter.17.cloned.1.call-done = f32[768,96]{0,1:T(8,128)} async-done(((f32[768,768]{0,1:T(8,128)}), f32[768,96]{0,1:T(8,128)}) %reduce-scatter.17.cloned.1.call-update) | async-done | bytes 294928 | tf_op jit(solution)/shard_map/reduce_scatter | solution.py:300
  1581.6 36.1 %reduce-scatter.21.cloned.1.call-done = f32[96,2]{1,0:T(8,128)} async-done(((f32[768,2]{1,0:T(8,128)}), f32[96,2]{1,0:T(8,128)}) %reduce-scatter.21.cloned.1.call-update) | async-done | bytes 784
  1619.9 36.2 %reduce-scatter.19.cloned.1.call-done = f32[96,192]{1,0:T(8,128)} async-done(((f32[768,192]{1,0:T(8,128)}), f32[96,192]{1,0:T(8,128)}) %reduce-scatter.19.cloned.1.call-update) | async-done | bytes 73744
  1657.7 56.8 %reduce-scatter.15.cloned.1.call-done = f32[96,2,768]{2,0,1:T(8,128)} async-done(((f32[768,2,768]{2,0,1:T(8,128)}), f32[96,2,768]{2,0,1:T(8,128)}) %reduce-scatter.15.cloned.1.call-update) | async-done | bytes 589840 | tf_op jit(solution)/shard_map/reduce_scatter | solution.py:299
  1716.2 44.5 %reduce-scatter.13.cloned.1.call-done = f32[96,3,192]{2,0,1:T(8,128)} async-done(((f32[768,3,192]{2,0,1:T(8,128)}), f32[96,3,192]{2,0,1:T(8,128)}) %reduce-scatter.13.cloned.1.call-update) | async-done | bytes 221200 | tf_op jit(solution)/shard_map/reduce_scatter | solution.py:297
  1769.4 13.3 copy.156
  1782.7 53.5 %psum.31 = f32[]{:T(128)} all-reduce(f32[]{:T(128)S(6)} %add.322), channel_id=1, replica_groups=mesh['batch'=8,'mp'=4] {'batch','mp'}, use_global_device_ids=true, to_apply=%region_46.47 | all-reduce | flops 1 | bytes 8 | tf_op jit(solution)/shard_map/psum | solution.py:307
  1845.8 123.3 %all-gather.15.cloned.1.call-done = f32[3816,768]{0,1:T(8,128)} async-done(((f32[3816,192]{0,1:T(8,128)}), f32[3816,768]{0,1:T(8,128)}) %all-gather.15.cloned.1.call-update) | async-done | bytes 11722768 | tf_op jit(solution)/shard_map/all_gather | solution.py:306
  1969.1 17.3 fusion.46
  1986.5 12.3 copy.167
  1998.8 22.2 %fusion.45 = f32[3816,768]{0,1:T(8,128)} fusion(f32[3816,768]{0,1:T(8,128)} %copy.139, f32[3816,768]{0,1:T(8,128)} %get-tuple-element.440, f32[3816,768]{0,1:T(8,128)} %copy.156, f32[3816,768]{0,1:T(8,128)} %copy.158), kind=kLoop, calls=%fused_computation.57 | loop fusion | flops 41029632 | bytes 58613760 | tf_op jit(solution)/shard_map/sub | solution.py:147
  2021.0 12.3 copy.165
  2033.3 12.4 copy.169
  (317 shorter events, 146.3 us)
Async XLA Ops:
  7.2 15.7 copy-start
  7.2 87.3 %all-gather.21.cloned.1.call-start = ((), (), s32[]{:S(2)}) async-start(), calls=%async_computation.18 | async-start | bytes 13271040 | tf_op jit(solution)/shard_map/all_gather | solution.py:181
  7.3 15.6 copy-start.52
  22.8 152.7 %all-gather.17.cloned.1.call-start = ((), (), s32[]{:S(2)}) async-start(), calls=%async_computation.16 | async-start | bytes 2949120 | tf_op jit(solution)/shard_map/all_gather | solution.py:195
  31.4 81.2 %copy-start.49 = (s32[1536]{0:T(1024)}, s32[1536]{0:T(1024)S(1)}, u32[]{:S(2)}) copy-start(s32[1536]{0:T(1024)S(1)} %fusion.104) | copy-start | bytes 18436
  112.5 12.4 copy-start.12
  112.5 13.2 copy-start.30
  112.5 13.9 copy-start.25
  123.7 18.1 copy-start.35
  124.8 103.6 %all-gather.11.cloned.1.call-start = ((), (), s32[]{:S(2)}) async-start(), calls=%async_computation.6 | async-start | bytes 2654208 | tf_op jit(solution)/shard_map/all_gather | solution.py:184
  125.7 414.4 %all-gather.19.cloned.1.call-start = ((), (), s32[]{:S(2)}) async-start(), calls=%async_computation.17 | async-start | bytes 23592960 | tf_op jit(solution)/shard_map/all_gather | solution.py:212
  150.8 64.7 %copy-start.10 = (bf16[192,768]{0,1:T(8,128)(2,1)}, bf16[192,768]{0,1:T(8,128)(2,1)S(1)}, u32[]{:S(2)}) copy-start(bf16[192,768]{0,1:T(8,128)(2,1)S(1)} %all_gather.36) | copy-start | bytes 884740
  151.5 27.8 %copy-start.19 = (f32[1536,32]{0,1:T(8,128)}, f32[1536,32]{0,1:T(8,128)S(1)}, u32[]{:S(2)}) copy-start(f32[1536,32]{0,1:T(8,128)S(1)} %get-tuple-element.486) | copy-start | bytes 589828
  151.5 27.8 %copy-start.21 = (f32[1536,32]{0,1:T(8,128)}, f32[1536,32]{0,1:T(8,128)S(1)}, u32[]{:S(2)}) copy-start(f32[1536,32]{0,1:T(8,128)S(1)} %get-tuple-element.487) | copy-start | bytes 589828
  218.5 355.9 %all-gather.13.cloned.1.call-start = ((), (), s32[]{:S(2)}) async-start(), calls=%async_computation.7 | async-start | bytes 1327104 | tf_op jit(solution)/shard_map/all_gather | solution.py:185
  219.3 532.1 %all-reduce.10.cloned.1.call-start = ((), (), s32[]{:S(2)}) async-start(), calls=%async_computation.8 | async-start | bytes 9437184 | tf_op jit(solution)/shard_map/psum | solution.py:222
  228.4 743.7 %copy-start.45 = (f32[768]{0:T(1024)}, f32[768]{0:T(1024)S(1)}, u32[]{:S(2)}) copy-start(f32[768]{0:T(1024)S(1)} %get-tuple-element.396) | copy-start | bytes 9220
  560.7 7.4 copy-start.2
  560.7 411.4 %copy-start.41 = (f32[1536]{0:T(1024)}, f32[1536]{0:T(1024)S(1)}, u32[]{:S(2)}) copy-start(f32[1536]{0:T(1024)S(1)} %broadcast_multiply_fusion.3) | copy-start | bytes 18436
  561.3 410.8 %copy-start.43 = (f32[1536]{0:T(1024)}, f32[1536]{0:T(1024)S(1)}, u32[]{:S(2)}) copy-start(f32[1536]{0:T(1024)S(1)} %fusion.101) | copy-start | bytes 18436
  580.6 380.8 %all-reduce.12.cloned.1.call-start = ((), (), s32[]{:S(2)}) async-start(), calls=%async_computation.9 | async-start | bytes 9437184 | tf_op jit(solution)/shard_map/psum | solution.py:262
  770.4 5.2 slice-start.1
  775.6 5.6 copy-start.6
  775.6 185.9 %copy-start.47 = (f32[1536]{0:T(1024)}, f32[1536]{0:T(1024)S(1)}, u32[]{:S(2)}) copy-start(f32[1536]{0:T(1024)S(1)} %negate_multiply_fusion.1) | copy-start | bytes 18436
  775.9 7.5 copy-start.16
  791.3 530.9 %all-reduce.14.cloned.1.call-start = ((), (), s32[]{:S(2)}) async-start(), calls=%async_computation.10 | async-start | bytes 9437184 | tf_op jit(solution)/shard_map/psum | solution.py:287
  972.1 5.8 copy-start.11
  979.4 164.0 %copy-start.20 = (f32[1536,32]{0,1:T(8,128)S(1)}, f32[1536,32]{0,1:T(8,128)}, u32[]{:S(2)}) copy-start(f32[1536,32]{0,1:T(8,128)} %copy-done.19) | copy-start | bytes 589828
  979.4 7.3 copy-start.4
  1027.4 5.6 copy-start.5
  1033.0 7.5 copy-start.4
  1081.5 5.6 copy-start.5
  1087.1 7.5 copy-start.4
  1135.5 5.6 copy-start.5
  1151.0 383.2 %reduce-scatter.11.cloned.1.call-start = ((), (), s32[]{:S(2)}) async-start(), calls=%async_computation.11 | async-start | bytes 35168256 | tf_op jit(solution)/shard_map/reduce_scatter | solution.py:296
  1345.6 7.6 copy-start.50
  1345.6 7.6 copy-start.51
  1345.6 9.0 copy-start.9
  1345.6 234.3 %reduce-scatter.17.cloned.1.call-start = ((), (), s32[]{:S(2)}) async-start(), calls=%async_computation.14 | async-start | bytes 2654208 | tf_op jit(solution)/shard_map/reduce_scatter | solution.py:300
  1353.1 6.9 copy-start.42
  1353.1 6.9 copy-start.44
  1353.1 6.9 copy-start.46
  1353.1 264.6 %reduce-scatter.21.cloned.1.call-start = ((), (), s32[]{:S(2)}) async-start(), calls=%async_computation.20 | async-start | bytes 442368
  1354.2 301.9 %reduce-scatter.19.cloned.1.call-start = ((), (), s32[]{:S(2)}) async-start(), calls=%async_computation.19 | async-start | bytes 884736
  1359.9 354.6 %reduce-scatter.15.cloned.1.call-start = ((), (), s32[]{:S(2)}) async-start(), calls=%async_computation.13 | async-start | bytes 5308416 | tf_op jit(solution)/shard_map/reduce_scatter | solution.py:299
  1375.4 385.3 %reduce-scatter.13.cloned.1.call-start = ((), (), s32[]{:S(2)}) async-start(), calls=%async_computation.12 | async-start | bytes 2654208 | tf_op jit(solution)/shard_map/reduce_scatter | solution.py:297
  1382.8 586.4 %all-gather.15.cloned.1.call-start = ((), (), s32[]{:S(2)}) async-start(), calls=%async_computation.15 | async-start | bytes 14745600 | tf_op jit(solution)/shard_map/all_gather | solution.py:306
  1769.3 67.6 %copy-start.13 = (f32[96,2,768]{2,1,0:T(2,128)S(1)}, f32[96,2,768]{2,1,0:T(2,128)}, u32[]{:S(2)}) copy-start(f32[96,2,768]{2,1,0:T(2,128)} %param.37) | copy-start | bytes 1769476
  1769.3 67.6 %copy-start.14 = (f32[96,2,768]{2,0,1:T(8,128)S(1)}, f32[96,2,768]{2,0,1:T(8,128)}, u32[]{:S(2)}) copy-start(f32[96,2,768]{2,0,1:T(8,128)} %reduce-scatter.15.cloned.1.call-done) | copy-start | bytes 1769476
  1769.3 67.6 %copy-start.31 = (f32[96,2,768]{2,1,0:T(2,128)S(1)}, f32[96,2,768]{2,1,0:T(2,128)}, u32[]{:S(2)}) copy-start(f32[96,2,768]{2,1,0:T(2,128)} %param.43) | copy-start | bytes 1769476
  1769.4 67.6 %copy-start.32 = (f32[96,2,768]{2,1,0:T(2,128)S(1)}, f32[96,2,768]{2,1,0:T(2,128)}, u32[]{:S(2)}) copy-start(f32[96,2,768]{2,1,0:T(2,128)} %param.49) | copy-start | bytes 1769476
  1782.7 58.6 %copy-start.54 = (f32[2,96]{1,0:T(2,128)S(1)}, f32[2,96]{1,0:T(2,128)}, u32[]{:S(2)}) copy-start(f32[2,96]{1,0:T(2,128)} %param.39) | copy-start | bytes 2308
  1782.7 58.6 %copy-start.55 = (f32[2,96]{1,0:T(2,128)S(1)}, f32[2,96]{1,0:T(2,128)}, u32[]{:S(2)}) copy-start(f32[2,96]{1,0:T(2,128)} %param.45) | copy-start | bytes 2308
  1782.7 58.6 %copy-start.56 = (f32[2,96]{1,0:T(2,128)S(1)}, f32[2,96]{1,0:T(2,128)}, u32[]{:S(2)}) copy-start(f32[2,96]{1,0:T(2,128)} %param.51) | copy-start | bytes 2308
  1782.7 59.2 %copy-start.36 = (f32[192,96]{1,0:T(8,128)S(1)}, f32[192,96]{1,0:T(8,128)}, u32[]{:S(2)}) copy-start(f32[192,96]{1,0:T(8,128)} %param.36) | copy-start | bytes 221188
  1782.7 60.9 %copy-start.24 = (f32[768,96]{0,1:T(8,128)S(1)}, f32[768,96]{0,1:T(8,128)}, u32[]{:S(2)}) copy-start(f32[768,96]{0,1:T(8,128)} %param.38) | copy-start | bytes 884740
  1782.7 60.9 %copy-start.27 = (f32[768,96]{0,1:T(8,128)S(1)}, f32[768,96]{0,1:T(8,128)}, u32[]{:S(2)}) copy-start(f32[768,96]{0,1:T(8,128)} %reduce-scatter.17.cloned.1.call-done) | copy-start | bytes 884740
  1782.7 60.9 %copy-start.37 = (f32[768,96]{0,1:T(8,128)S(1)}, f32[768,96]{0,1:T(8,128)}, u32[]{:S(2)}) copy-start(f32[768,96]{0,1:T(8,128)} %param.44) | copy-start | bytes 884740
  1837.0 6.6 copy-start.38
  1837.0 7.7 copy-start.26
  1837.0 7.7 copy-start.28
  1837.0 7.7 copy-start.39
  1837.0 7.7 copy-start.40
  2033.3 12.4 copy-start.1
  (21 other events, 49.3 us)
Sparse Core Ops, SparseCore 0:
  22.9 71.4 all-gather.20
  125.0 50.4 all-gather.16
  178.0 27.8 all-gather.10
  218.6 321.3 all-gather.18
  542.4 22.8 all-gather.12
  580.7 170.5 all-reduce.9
  791.4 170.0 all-reduce.11
  1151.1 170.9 all-reduce.13
  1345.7 188.4 reduce-scatter.10
  1537.4 42.4 reduce-scatter.16
  1583.9 33.8 reduce-scatter.20
  1621.1 34.9 reduce-scatter.18
  1660.5 53.9 reduce-scatter.14
  1718.2 42.4 reduce-scatter.12
  1762.8 206.3 all-gather.14
